TPU v7x, 32 devices: a whole 2x2x4 slice. The times are simulated.
32 devices in a mesh: row: 8 (over z, x), col: 4 (over y, core).
Axes of the slice: x: 2, y: 2, z: 4, core: 2. Of those that a mesh axis runs over, the one named last changes fastest.
Arguments:
- tokens: bfloat16 [4096, 768], P(('row', 'col')), may hold values from -6 to 6
- w_qkv: bfloat16 [768, 3, 768], P('row', None, 'col'), may hold values from -0.21875 to 0.21875
- w_out: bfloat16 [768, 768], P('col', 'row'), may hold values from -2.5 to 2.5
- w_gate_up: bfloat16 [768, 2, 3072], P('row', None, 'col'), may hold values from -0.21875 to 0.21875
- w_down: bfloat16 [3072, 768], P('col', 'row'), may hold values from -0.109375 to 0.109375
- gain1: float32 [768], replicated, may hold values from 0.1 to 1.9
- bias1: float32 [768], replicated, may hold values from -1.8 to 1.8
- gain2: float32 [768], replicated, may hold values from 0.1 to 1.9
- bias2: float32 [768], replicated, may hold values from -1.8 to 1.8
- cotangent: bfloat16 [4096, 768], P(('row', 'col')), may hold values from -6 to 6
- seq_lengths: int32 [3], replicated, may hold values from 512 to 2048, as said below
- packed_order: int32 [4096], replicated, may hold values from 0 to 4095, each once
Outputs:
- output: bfloat16 [4096, 768], P(('row', 'col'))
- grad_tokens: float32 [4096, 768], P(('row', 'col'))
- grad_w_qkv: float32 [768, 3, 768], P('row', None, 'col')
- grad_w_out: float32 [768, 768], P('col', 'row')
- grad_w_gate_up: float32 [768, 2, 3072], P('row', None, 'col')
- grad_w_down: float32 [3072, 768], P('col', 'row')
- grad_gain1: float32 [768], replicated
- grad_bias1: float32 [768], replicated
- grad_gain2: float32 [768], replicated
- grad_bias2: float32 [768], replicated
Inputs may be any that keep to these rules, and one draw needn't show every extreme that they name: `seq_lengths`: 3 lengths that sum to 4096; the longest is exactly 2048.
All inputs are finite; a program needn't handle non-finite values.
Results may differ from a plain program's by a relative error of at most 0.024.
Values may be sent and summed in bfloat16 or wider, within the bound.
No kernel may reach another device: no remote copies, remote signals or barrier semaphores. Data moves between devices by JAX's collectives and lax.ppermute only.
A program may use at most 512 MiB of HBM per device.

v0:
```python
import math
import jax
import jax.numpy as jnp
from jax import lax
from jax.sharding import PartitionSpec as P

HEAD = 64
ROPE_BASE = 1000.0
NORM_EPS = 1e-12
MASKED = -1e30


def token_layout(seq_lengths, packed_order):
    seq_ends = jnp.cumsum(seq_lengths)
    seq_starts = seq_ends - seq_lengths
    seq_id = jnp.sum((packed_order[:, None] >= seq_ends[None, :]).astype(jnp.int32), axis=1)
    member = seq_id[:, None] == jnp.arange(seq_lengths.shape[0], dtype=jnp.int32)[None, :]
    start_of = jnp.sum(jnp.where(member, seq_starts[None, :], 0), axis=1)
    return (seq_id, packed_order - start_of)


def rope_tables(positions, head):
    half = head // 2
    freqs = ROPE_BASE ** (-jnp.arange(half, dtype=jnp.float32) * 2.0 / head)
    angles = positions.astype(jnp.float32)[:, None] * freqs[None, :]
    return (jnp.cos(angles), jnp.sin(angles))


def rotate(field, cosine, sine):
    half = field.shape[-1] // 2
    first = field[..., :half]
    second = field[..., half:]
    cos_b = cosine[:, None, :]
    sin_b = sine[:, None, :]
    return jnp.concatenate(
        [first * cos_b - second * sin_b, second * cos_b + first * sin_b], axis=-1
    )


def rotate_back(field, cosine, sine):
    half = field.shape[-1] // 2
    first = field[..., :half]
    second = field[..., half:]
    cos_b = cosine[:, None, :]
    sin_b = sine[:, None, :]
    return jnp.concatenate(
        [first * cos_b + second * sin_b, second * cos_b - first * sin_b], axis=-1
    )


def norm_forward(values, gain, bias):
    centered = values - jnp.mean(values, axis=-1, keepdims=True)
    inverse = lax.rsqrt(jnp.mean(centered * centered, axis=-1, keepdims=True) + NORM_EPS)
    normed = centered * inverse
    return (normed * gain + bias, normed, inverse)


def norm_backward(grad_out, normed, inverse, gain):
    scaled = grad_out * gain
    grad_in = inverse * (
        scaled
        - jnp.mean(scaled, axis=-1, keepdims=True)
        - normed * jnp.mean(scaled * normed, axis=-1, keepdims=True)
    )
    return (grad_in, jnp.sum(grad_out * normed, axis=0), jnp.sum(grad_out, axis=0))


def gather_rows(rows):
    return lax.all_gather(rows, "col", axis=0, tiled=True)


def gather_grads(rows):
    return lax.all_gather(rows, "col", axis=0, tiled=True)


def column_sum(left, product):
    return lax.psum_scatter(
        product(left).astype(jnp.bfloat16), "col", scatter_dimension=0, tiled=True
    ).astype(jnp.float32)


def score_block(queries, seg_queries, key_rows, seg_keys, scale):
    count = key_rows.shape[0]
    heads = queries.shape[1]
    head = queries.shape[2]
    scores = (
        jnp.einsum(
            "qhd,khd->hqk",
            queries,
            key_rows.reshape(count, heads, head),
            preferred_element_type=jnp.float32,
        )
        * scale
    )
    same = seg_queries[:, None] == seg_keys[None, :]
    return (scores, same)


def probabilities(queries, seg_queries, log_total, key_rows, seg_keys, scale):
    scores, same = score_block(queries, seg_queries, key_rows, seg_keys, scale)
    return jnp.where(same[None], jnp.exp(scores - log_total[..., None]), 0.0)


def score_grads(probs, grad_heads, delta, value_rows):
    count = value_rows.shape[0]
    heads = grad_heads.shape[1]
    head = grad_heads.shape[2]
    grad_probs = jnp.einsum(
        "qhd,khd->hqk",
        grad_heads,
        value_rows.reshape(count, heads, head),
        preferred_element_type=jnp.float32,
    )
    return (probs * (grad_probs - delta[..., None])).astype(jnp.bfloat16)


def local(
    tokens,
    w_qkv,
    w_out,
    w_gate_up,
    w_down,
    gain1,
    bias1,
    gain2,
    bias2,
    cotangent,
    seq_lengths,
    packed_order,
):
    row_index = lax.axis_index("row")
    shards = lax.axis_size("row")
    full_qkv, full_out, full_gate_up, full_down = (
        lax.all_gather(w_qkv, "row", axis=0, tiled=True),
        lax.all_gather(w_out, "row", axis=1, tiled=True),
        lax.all_gather(w_gate_up, "row", axis=0, tiled=True),
        lax.all_gather(w_down, "row", axis=1, tiled=True),
    )
    seq_all, positions = token_layout(seq_lengths, packed_order)
    token_block = gather_rows(tokens)
    group = token_block.shape[0]
    first_slot = row_index * group
    seg_rows = lax.dynamic_slice_in_dim(seq_all, first_slot, group, 0)
    cosine, sine = rope_tables(lax.dynamic_slice_in_dim(positions, first_slot, group, 0), HEAD)
    width = full_qkv.shape[2]
    local_heads = width // HEAD
    scale = 1.0 / math.sqrt(HEAD)
    mixed = jnp.einsum("td,dce->tce", token_block, full_qkv, preferred_element_type=jnp.float32)
    query_bf = rotate(mixed[:, 0].reshape(group, local_heads, HEAD), cosine, sine).astype(
        jnp.bfloat16
    )
    key_bf = (
        rotate(mixed[:, 1].reshape(group, local_heads, HEAD), cosine, sine)
        .astype(jnp.bfloat16)
        .reshape(group, width)
    )
    value_bf = mixed[:, 2].astype(jnp.bfloat16)
    run_max = jnp.full((local_heads, group), MASKED, jnp.float32)
    key_piece = lax.all_gather(key_bf, "row", axis=0, tiled=True)
    value_piece = lax.all_gather(value_bf, "row", axis=0, tiled=True)
    count = key_piece.shape[0]
    seg_keys = seq_all
    scores, same = score_block(query_bf, seg_rows, key_piece, seg_keys, scale)
    new_max = jnp.maximum(run_max, jnp.max(jnp.where(same[None], scores, MASKED), axis=-1))
    weights_now = jnp.where(same[None], jnp.exp(scores - new_max[..., None]), 0.0)
    new_total = jnp.sum(weights_now, axis=-1)
    new_acc = jnp.einsum(
        "hqk,khd->hqd",
        weights_now.astype(jnp.bfloat16),
        value_piece.reshape(count, local_heads, HEAD),
        preferred_element_type=jnp.float32,
    )
    context = new_acc / new_total[..., None]
    log_total = new_max + jnp.log(new_total)
    context_bf = jnp.transpose(context, (1, 0, 2)).reshape(group, width).astype(jnp.bfloat16)

    def out_product(rows):
        return jnp.dot(rows, full_out, preferred_element_type=jnp.float32)

    attn_out = column_sum(context_bf, out_product)
    residual1 = tokens.astype(jnp.float32) + attn_out
    hidden1, normed1, inverse1 = norm_forward(residual1, gain1, bias1)
    hidden_block = gather_rows(hidden1.astype(jnp.bfloat16))
    gate_up = jnp.einsum(
        "td,dcf->tcf", hidden_block, full_gate_up, preferred_element_type=jnp.float32
    )
    up = gate_up[:, 0]
    gate = gate_up[:, 1]
    sigma = jax.nn.sigmoid(gate)
    inner = (gate * sigma * up).astype(jnp.bfloat16)

    def down_product(rows):
        return jnp.dot(rows, full_down, preferred_element_type=jnp.float32)

    ffn_out = column_sum(inner, down_product)
    residual2 = hidden1 + ffn_out
    result, normed2, inverse2 = norm_forward(residual2, gain2, bias2)
    grad_res2, grad_gain2, grad_bias2 = norm_backward(
        cotangent.astype(jnp.float32), normed2, inverse2, gain2
    )
    grad_ffn = gather_grads(grad_res2.astype(jnp.bfloat16))
    grad_inner = lax.dot_general(
        grad_ffn, full_down, (((1,), (1,)), ((), ())), preferred_element_type=jnp.float32
    )
    grad_down = lax.dot_general(
        inner, grad_ffn, (((0,), (0,)), ((), ())), preferred_element_type=jnp.float32
    )
    grad_up = grad_inner * gate * sigma
    grad_gate = grad_inner * up * sigma * (1.0 + gate * (1.0 - sigma))
    grad_gate_up = jnp.stack([grad_up, grad_gate], axis=1).astype(jnp.bfloat16)

    def gate_up_back(rows):
        return jnp.einsum("tcf,dcf->td", rows, full_gate_up, preferred_element_type=jnp.float32)

    grad_hidden1 = grad_res2 + column_sum(grad_gate_up, gate_up_back)
    grad_wgu = jnp.einsum(
        "td,tcf->dcf", hidden_block, grad_gate_up, preferred_element_type=jnp.float32
    )
    grad_res1, grad_gain1, grad_bias1 = norm_backward(grad_hidden1, normed1, inverse1, gain1)
    grad_attn = gather_grads(grad_res1.astype(jnp.bfloat16))
    grad_wo = lax.dot_general(
        context_bf, grad_attn, (((0,), (0,)), ((), ())), preferred_element_type=jnp.float32
    )
    grad_context_bf = lax.dot_general(
        grad_attn, full_out, (((1,), (1,)), ((), ())), preferred_element_type=jnp.float32
    ).astype(jnp.bfloat16)
    grad_heads = grad_context_bf.reshape(group, local_heads, HEAD)
    delta = jnp.sum(jnp.transpose(grad_heads, (1, 0, 2)).astype(jnp.float32) * context, axis=-1)
    key_all, value_all = (
        lax.all_gather(key_bf, "row", axis=0, tiled=True),
        lax.all_gather(value_bf, "row", axis=0, tiled=True),
    )
    tokens_total = key_all.shape[0]
    per_turn = group * math.gcd(shards, max(1, 2048 // group))
    turns = tokens_total // per_turn

    def turn_terms(turn):
        begin = turn * per_turn
        key_rows = lax.dynamic_slice_in_dim(key_all, begin, per_turn, 0)
        value_rows = lax.dynamic_slice_in_dim(value_all, begin, per_turn, 0)
        seg_keys = lax.dynamic_slice_in_dim(seq_all, begin, per_turn, 0)
        probs = probabilities(query_bf, seg_rows, log_total, key_rows, seg_keys, scale)
        grad_scores = score_grads(probs, grad_heads, delta, value_rows)
        return (begin, key_rows, probs, grad_scores)

    def query_term(grad_scores, key_rows):
        return jnp.einsum(
            "hqk,khd->qhd",
            grad_scores,
            key_rows.reshape(per_turn, local_heads, HEAD),
            preferred_element_type=jnp.float32,
        )

    empty_query = jnp.zeros((group, local_heads, HEAD), jnp.float32)

    def key_turn(turn, carry):
        grad_query, grad_keys, grad_values = carry
        begin, key_rows, probs, grad_scores = turn_terms(turn)
        grad_query = grad_query + query_term(grad_scores, key_rows)
        key_term = jnp.einsum(
            "hqk,qhd->khd", grad_scores, query_bf, preferred_element_type=jnp.float32
        ).reshape(per_turn, width)
        value_term = jnp.einsum(
            "hqk,qhd->khd",
            probs.astype(jnp.bfloat16),
            grad_heads,
            preferred_element_type=jnp.float32,
        ).reshape(per_turn, width)
        grad_keys = lax.dynamic_update_slice_in_dim(grad_keys, key_term, begin, 0)
        grad_values = lax.dynamic_update_slice_in_dim(grad_values, value_term, begin, 0)
        return (grad_query, grad_keys, grad_values)

    empty_keys = jnp.zeros((tokens_total, width), jnp.float32)
    grad_query, grad_keys_all, grad_values_all = lax.fori_loop(
        0, turns, key_turn, (empty_query, empty_keys, empty_keys)
    )
    grad_key_rows, grad_value_rows = (
        lax.psum_scatter(grad_keys_all, "row", scatter_dimension=0, tiled=True),
        lax.psum_scatter(grad_values_all, "row", scatter_dimension=0, tiled=True),
    )
    grad_query_raw = rotate_back(grad_query * scale, cosine, sine).reshape(group, width)
    grad_key_raw = rotate_back(
        grad_key_rows.reshape(group, local_heads, HEAD) * scale, cosine, sine
    ).reshape(group, width)
    grad_mixed = jnp.stack([grad_query_raw, grad_key_raw, grad_value_rows], axis=1).astype(
        jnp.bfloat16
    )

    def qkv_back(rows):
        return jnp.einsum("tce,dce->td", rows, full_qkv, preferred_element_type=jnp.float32)

    grad_tokens = grad_res1 + column_sum(grad_mixed, qkv_back)
    grad_wqkv = jnp.einsum(
        "td,tce->dce", token_block, grad_mixed, preferred_element_type=jnp.float32
    )
    grad_w_qkv, grad_w_out, grad_w_gate_up, grad_w_down = (
        lax.psum_scatter(grad_wqkv, "row", scatter_dimension=0, tiled=True),
        lax.psum_scatter(grad_wo, "row", scatter_dimension=1, tiled=True),
        lax.psum_scatter(grad_wgu, "row", scatter_dimension=0, tiled=True),
        lax.psum_scatter(grad_down, "row", scatter_dimension=1, tiled=True),
    )
    norm_gain1, norm_bias1, norm_gain2, norm_bias2 = lax.psum(
        (grad_gain1, grad_bias1, grad_gain2, grad_bias2), ("row", "col")
    )
    return (
        result.astype(jnp.bfloat16),
        grad_tokens,
        grad_w_qkv,
        grad_w_out,
        grad_w_gate_up,
        grad_w_down,
        norm_gain1,
        norm_bias1,
        norm_gain2,
        norm_bias2,
    )


def solution(mesh):
    placed = (
        P(("row", "col"), None),
        P("row", None, "col"),
        P("col", "row"),
        P("row", None, "col"),
        P("col", "row"),
        P(),
        P(),
        P(),
        P(),
        P(("row", "col"), None),
        P(),
        P(),
    )
    return jax.shard_map(
        local,
        mesh=mesh,
        in_specs=placed,
        out_specs=(
            P(("row", "col"), None),
            P(("row", "col"), None),
            P("row", None, "col"),
            P("col", "row"),
            P("row", None, "col"),
            P("col", "row"),
            P(),
            P(),
            P(),
            P(),
        ),
        check_vma=False,
    )
```

profile of v0, /device:TPU:0, one launch (start us, length us, event | category | flops | bytes accessed | tf_op | source)
XLA Modules:
  0.0 918.4 jit_solution(15256059629411682818)
XLA Ops:
  9.8 38.8 %all_gather.33 = bf16[768,3,192]{2,1,0:T(4,128)(2,1)S(1)} all-gather(bf16[96,3,192]{2,1,0:T(4,128)(2,1)S(1)} %copy.45), channel_id=1, replica_groups=mesh['row'=8,'col'=4] {'row'}, dimensions={0}, use_global_device_ids=true | all-gather | bytes 995328 | tf_op jit(solution)/shard_map/all_gather | solution.py:134
  49.5 8.8 all_gather.32
  64.3 31.8 %all_gather.36 = bf16[192,768]{0,1:T(8,128)(2,1)S(1)} all-gather(bf16[192,96]{0,1:T(8,128)(2,1)S(1)} %copy.47), channel_id=1, replica_groups=mesh['row'=8,'col'=4] {'row'}, dimensions={1}, use_global_device_ids=true | all-gather | bytes 331776 | tf_op jit(solution)/shard_map/all_gather | solution.py:135
  96.1 11.8 %all-gather.6.cloned.1.call-done = bf16[4096,192]{0,1:T(8,128)(2,1)} async-done(((bf16[512,192]{0,1:T(8,128)(2,1)}), bf16[4096,192]{0,1:T(8,128)(2,1)}) %all-gather.6.cloned.1.call-update) | async-done | bytes 1572880 | tf_op jit(solution)/shard_map/all_gather | solution.py:159
  107.9 12.5 %select_reduce_fusion = (f32[3,512]{1,0:T(4,128)S(1)}, f32[3,512,4096]{2,1,0:T(8,128)}) fusion(pred[512,4096]{1,0:T(8,128)(4,1)S(1)} %broadcast_compare_fusion.1, bf16[4096,3,64]{0,2,1:T(8,128)(2,1)} %bitcast.162, bf16[512,3,32]{0,2,1:T(8,128)(2,1)S(1)} %get-tuple-element.336, bf16[512,3,32]{0,2,1:T(8,128)(2,1)S(1)} %get-tuple-element.335), kind=kOutput, calls=%fused_computation.16 | convolution fusion | flops 824572416 | bytes 29038592 | tf_op jit(solution)/shard_map/qhd,khd->hqk/dot_general | solution.py:87
  120.4 12.0 %fusion.8 = f32[3,512]{1,0:T(4,128)S(1)} fusion(f32[3,512,4096]{2,1,0:T(8,128)} %get-tuple-element.347, f32[3,512]{1,0:T(4,128)S(1)} %broadcast_maximum_fusion, pred[512,4096]{1,0:T(8,128)(4,1)S(1)} %broadcast_compare_fusion.1), kind=kLoop, calls=%fused_computation.17 | loop fusion | flops 25164288 | bytes 27275264 | tf_op jit(solution)/shard_map/reduce_sum | solution.py:166
  132.4 21.2 %all-gather.12.cloned.1.call-done = bf16[4096,1,192]{0,2,1:T(8,128)(2,1)} async-done(((bf16[512,1,192]{0,2,1:T(8,128)(2,1)}), bf16[4096,1,192]{0,2,1:T(8,128)(2,1)}) %all-gather.12.cloned.1.call-update) | async-done | bytes 1572880 | tf_op jit(solution)/shard_map/all_gather | solution.py:160
  153.6 12.0 %fusion.29 = (bf16[512,3,64]{0,2,1:T(8,128)(2,1)S(1)}, f32[3,512,64]{1,2,0:T(8,128)}) fusion(f32[512,3]{0,1:T(4,128)S(1)} %bitcast.183, bf16[4096,3,64]{0,2,1:T(8,128)(2,1)} %bitcast.163, f32[3,512,4096]{2,1,0:T(8,128)} %get-tuple-element.347, f32[3,512]{1,0:T(4,128)S(1)} %broadcast_maximum_fusion, pred[512,4096]{1,0:T(8,128)(4,1)S(1)} %broadcast_compare_fusion.1), kind=kOutput, calls=%fused_computation.58 | convolution fusion | flops 830668800 | bytes 29437952 | tf_op jit(solution)/shard_map/hqk,khd->hqd/dot_general | solution.py:167
  169.4 19.2 %reduce-scatter.15.cloned.1.call-done = bf16[128,768]{1,0:T(8,128)(2,1)} async-done(((bf16[512,768]{1,0:T(8,128)(2,1)}), bf16[128,768]{1,0:T(8,128)(2,1)}) %reduce-scatter.15.cloned.1.call-update) | async-done | bytes 196624 | tf_op jit(solution)/shard_map/reduce_scatter | solution.py:77
  191.8 8.4 all_gather.37
  200.2 43.2 %all-gather.8.cloned.1.call-done = bf16[768,2,768]{2,0,1:T(8,128)(2,1)} async-done(((bf16[96,2,768]{2,0,1:T(8,128)(2,1)}), bf16[768,2,768]{2,0,1:T(8,128)(2,1)}) %all-gather.8.cloned.1.call-update) | async-done | bytes 2359312 | tf_op jit(solution)/shard_map/all_gather | solution.py:136
  248.6 36.7 %all-gather.10.cloned.1.call-done = bf16[768,768]{0,1:T(8,128)(2,1)} async-done(((bf16[768,96]{0,1:T(8,128)(2,1)}), bf16[768,768]{0,1:T(8,128)(2,1)}) %all-gather.10.cloned.1.call-update) | async-done | bytes 1179664 | tf_op jit(solution)/shard_map/all_gather | solution.py:137
  288.3 22.1 %reduce-scatter.17.cloned.1.call-done = bf16[128,768]{1,0:T(8,128)(2,1)} async-done(((bf16[512,768]{1,0:T(8,128)(2,1)}), bf16[128,768]{1,0:T(8,128)(2,1)}) %reduce-scatter.17.cloned.1.call-update) | async-done | bytes 196624 | tf_op jit(solution)/shard_map/reduce_scatter | solution.py:77
  313.7 8.2 all_gather.40
  328.2 23.7 %reduce-scatter.19.cloned.1.call-done = bf16[128,768]{1,0:T(8,128)(2,1)} async-done(((bf16[512,768]{1,0:T(8,128)(2,1)}), bf16[128,768]{1,0:T(8,128)(2,1)}) %reduce-scatter.19.cloned.1.call-update) | async-done | bytes 196624 | tf_op jit(solution)/shard_map/reduce_scatter | solution.py:77
  368.2 58.9 %while.18 = (s32[]{:T(128)}, f32[512,3,64]{0,2,1:T(8,128)S(1)}, f32[4096,192]{0,1:T(8,128)}, f32[4096,192]{0,1:T(8,128)}, bf16[4096,192]{0,1:T(8,128)(2,1)S(1)},...) while((s32[]{:T(128)}, f32[512,3,64]{0,2,1:T(8,128)S(1)}, ...), condition=%wide.region_18.19_spmd.clone, body=%wide.region_17.18_spmd.clone.sunk | while | flops 2045968384 | bytes 107786520 | solution.py:274
  434.6 68.0 %reduce-scatter.21.cloned.1.call-done = f32[512,192]{0,1:T(8,128)} async-done(((f32[4096,192]{0,1:T(8,128)}), f32[512,192]{0,1:T(8,128)}) %reduce-scatter.21.cloned.1.call-update) | async-done | bytes 393232 | tf_op jit(solution)/shard_map/reduce_scatter | solution.py:278
  503.8 76.9 %reduce-scatter.23.cloned.1.call-done = f32[512,192]{0,1:T(8,128)} async-done(((f32[4096,192]{0,1:T(8,128)}), f32[512,192]{0,1:T(8,128)}) %reduce-scatter.23.cloned.1.call-update) | async-done | bytes 393232 | tf_op jit(solution)/shard_map/reduce_scatter | solution.py:279
  590.5 40.1 %all-reduce = (f32[768]{0:T(1024)}, f32[768]{0:T(1024)}, f32[768]{0:T(1024)}, f32[768]{0:T(1024)}) all-reduce(f32[768]{0:T(1024)S(1)} %get-tuple-element.283, f32[768]{0:T(1024)S(1)} %get-tuple-element.288, f32[768]{0:T(1024)S(1)} %copy-done.34, f32[768]{0:T(1024)S(1)} %copy-done.35), channel_id=1, replica_groups=mesh['row'=8,'col'=4] {'row','col'}, use_global_device_ids=true, to_apply=%region_27.28 | all-reduce | flops 3072 | bytes 24576 | tf_op jit(solution)/shard_map/psum | solution.py:302
  630.6 15.3 %reduce-scatter.33.cloned.1.call-done = f32[96,192]{1,0:T(8,128)} async-done(((f32[768,192]{1,0:T(8,128)}), f32[96,192]{1,0:T(8,128)}) %reduce-scatter.33.cloned.1.call-update) | async-done | bytes 73744
  647.6 96.2 %reduce-scatter.27.cloned.1.call-done = f32[96,2,768]{2,0,1:T(8,128)} async-done(((f32[768,2,768]{2,0,1:T(8,128)}), f32[96,2,768]{2,0,1:T(8,128)}) %reduce-scatter.27.cloned.1.call-update) | async-done | bytes 589840 | tf_op jit(solution)/shard_map/reduce_scatter | solution.py:299
  746.1 23.1 %reduce-scatter.25.cloned.1.call-done = bf16[128,768]{1,0:T(8,128)(2,1)} async-done(((bf16[512,768]{1,0:T(8,128)(2,1)}), bf16[128,768]{1,0:T(8,128)(2,1)}) %reduce-scatter.25.cloned.1.call-update) | async-done | bytes 196624 | tf_op jit(solution)/shard_map/reduce_scatter | solution.py:77
  771.0 69.1 %reduce-scatter.31.cloned.1.call-done = f32[96,576]{1,0:T(8,128)} async-done(((f32[768,576]{1,0:T(8,128)}), f32[96,576]{1,0:T(8,128)}) %reduce-scatter.31.cloned.1.call-update) | async-done | bytes 221200
  842.0 69.8 %reduce-scatter.29.cloned.1.call-done = f32[768,96]{0,1:T(8,128)} async-done(((f32[768,768]{0,1:T(8,128)}), f32[768,96]{0,1:T(8,128)}) %reduce-scatter.29.cloned.1.call-update) | async-done | bytes 294928 | tf_op jit(solution)/shard_map/reduce_scatter | solution.py:300
  (200 shorter events, 134.8 us)
Async XLA Ops:
  7.2 100.7 %all-gather.6.cloned.1.call-start = ((), (), s32[]{:S(2)}) async-start(), calls=%async_computation.10 | async-start | bytes 1769472 | tf_op jit(solution)/shard_map/all_gather | solution.py:159
  62.0 91.6 %all-gather.12.cloned.1.call-start = ((), (), s32[]{:S(2)}) async-start(), calls=%async_computation.21 | async-start | bytes 1769472 | tf_op jit(solution)/shard_map/all_gather | solution.py:160
  62.7 125.8 %reduce-scatter.15.cloned.1.call-start = ((), (), s32[]{:S(2)}) async-start(), calls=%async_computation.11 | async-start | bytes 983040 | tf_op jit(solution)/shard_map/reduce_scatter | solution.py:77
  167.0 76.4 %all-gather.8.cloned.1.call-start = ((), (), s32[]{:S(2)}) async-start(), calls=%async_computation.12 | async-start | bytes 2654208 | tf_op jit(solution)/shard_map/all_gather | solution.py:136
  168.8 116.5 %all-gather.10.cloned.1.call-start = ((), (), s32[]{:S(2)}) async-start(), calls=%async_computation.13 | async-start | bytes 1327104 | tf_op jit(solution)/shard_map/all_gather | solution.py:137
  169.3 141.1 %reduce-scatter.17.cloned.1.call-start = ((), (), s32[]{:S(2)}) async-start(), calls=%async_computation.14 | async-start | bytes 983040 | tf_op jit(solution)/shard_map/reduce_scatter | solution.py:77
  248.6 64.2 %copy-start.7 = (bf16[512,768]{1,0:T(8,128)(2,1)}, bf16[512,768]{1,0:T(8,128)(2,1)S(1)}, u32[]{:S(2)}) copy-start(bf16[512,768]{1,0:T(8,128)(2,1)S(1)} %multiply_convert_fusion.2) | copy-start | bytes 2359300
  248.6 63.4 %copy-start.20 = (bf16[128,768]{1,0:T(8,128)(2,1)S(1)}, bf16[128,768]{1,0:T(8,128)(2,1)}, u32[]{:S(2)}) copy-start(bf16[128,768]{1,0:T(8,128)(2,1)} %param.23) | copy-start | bytes 589828
  248.6 64.2 %copy-start.36 = (f32[768]{0:T(1024)S(1)}, f32[768]{0:T(1024)}, u32[]{:S(2)}) copy-start(f32[768]{0:T(1024)} %param.22) | copy-start | bytes 9220
  288.3 63.7 %reduce-scatter.19.cloned.1.call-start = ((), (), s32[]{:S(2)}) async-start(), calls=%async_computation.15 | async-start | bytes 983040 | tf_op jit(solution)/shard_map/reduce_scatter | solution.py:77
  328.1 174.4 %reduce-scatter.21.cloned.1.call-start = ((), (), s32[]{:S(2)}) async-start(), calls=%async_computation.16 | async-start | bytes 3538944 | tf_op jit(solution)/shard_map/reduce_scatter | solution.py:278
  427.2 153.5 %reduce-scatter.23.cloned.1.call-start = ((), (), s32[]{:S(2)}) async-start(), calls=%async_computation.17 | async-start | bytes 3538944 | tf_op jit(solution)/shard_map/reduce_scatter | solution.py:279
  427.9 218.0 %reduce-scatter.33.cloned.1.call-start = ((), (), s32[]{:S(2)}) async-start(), calls=%async_computation.23 | async-start | bytes 884736
  429.7 314.1 %reduce-scatter.27.cloned.1.call-start = ((), (), s32[]{:S(2)}) async-start(), calls=%async_computation.19 | async-start | bytes 5308416 | tf_op jit(solution)/shard_map/reduce_scatter | solution.py:299
  434.5 69.1 %copy-start.22 = (f32[512,32]{0,1:T(8,128)S(1)}, f32[512,32]{0,1:T(8,128)}, u32[]{:S(2)}) copy-start(f32[512,32]{0,1:T(8,128)} %copy-done.21) | copy-start | bytes 196612
  434.5 69.1 %copy-start.24 = (f32[512,32]{0,1:T(8,128)S(1)}, f32[512,32]{0,1:T(8,128)}, u32[]{:S(2)}) copy-start(f32[512,32]{0,1:T(8,128)} %copy-done.23) | copy-start | bytes 196612
  434.5 147.9 %copy-start.10 = (bf16[768,3,192]{0,2,1:T(8,128)(2,1)S(1)}, bf16[768,3,192]{0,2,1:T(8,128)(2,1)}, u32[]{:S(2)}) copy-start(bf16[768,3,192]{0,2,1:T(8,128)(2,1)} %copy-done.9) | copy-start | bytes 2654212
  434.5 334.8 %reduce-scatter.25.cloned.1.call-start = ((), (), s32[]{:S(2)}) async-start(), calls=%async_computation.18 | async-start | bytes 983040 | tf_op jit(solution)/shard_map/reduce_scatter | solution.py:77
  503.7 80.4 %copy-start.26 = (bf16[512,3,64]{0,2,1:T(8,128)(2,1)}, bf16[512,3,64]{0,2,1:T(8,128)(2,1)S(1)}, u32[]{:S(2)}) copy-start(bf16[512,3,64]{0,2,1:T(8,128)(2,1)S(1)} %pad_maximum_fusion.8) | copy-start | bytes 589828
  503.8 80.7 %copy-start.14 = (bf16[512,768]{1,0:T(8,128)(2,1)S(1)}, bf16[512,768]{1,0:T(8,128)(2,1)}, u32[]{:S(2)}) copy-start(bf16[512,768]{1,0:T(8,128)(2,1)} %copy-done.13) | copy-start | bytes 2359300
  503.8 80.4 %copy-start.27 = (bf16[512,3,64]{0,2,1:T(8,128)(2,1)}, bf16[512,3,64]{0,2,1:T(8,128)(2,1)S(1)}, u32[]{:S(2)}) copy-start(bf16[512,3,64]{0,2,1:T(8,128)(2,1)S(1)} %pad_maximum_fusion.9) | copy-start | bytes 589828
  584.2 255.8 %reduce-scatter.31.cloned.1.call-start = ((), (), s32[]{:S(2)}) async-start(), calls=%async_computation.22 | async-start | bytes 2211840
  588.1 323.7 %reduce-scatter.29.cloned.1.call-start = ((), (), s32[]{:S(2)}) async-start(), calls=%async_computation.20 | async-start | bytes 2654208 | tf_op jit(solution)/shard_map/reduce_scatter | solution.py:300
  590.5 178.8 %copy-start.17 = (f32[128,768]{1,0:T(8,128)S(1)}, f32[128,768]{1,0:T(8,128)}, u32[]{:S(2)}) copy-start(f32[128,768]{1,0:T(8,128)} %get-tuple-element.320) | copy-start | bytes 1179652
  (33 other events, 386.7 us)
Sparse Core Ops, SparseCore 0:
  62.1 45.7 all-gather.5
  110.5 43.0 all-gather.11
  167.1 21.4 reduce-scatter.14
  191.4 51.9 all-gather.7
  245.7 39.5 all-gather.9
  288.4 22.0 reduce-scatter.16
  328.3 23.6 reduce-scatter.18
  427.3 75.2 reduce-scatter.20
  506.6 74.0 reduce-scatter.22
  584.2 61.6 reduce-scatter.32
  649.6 94.1 reduce-scatter.26
  746.2 23.0 reduce-scatter.24
  773.1 66.8 reduce-scatter.30
  843.9 67.8 reduce-scatter.28
where the time goes:
time: 919 us; the launch traced here: 918 us
  waiting for transfers between devices  598 us (65%)
  blocking collectives  144 us (16%)
  matrix products  101 us (11%)
  other arithmetic  31.8 us (3%)
  local copies, waits for them, and re-layouts  27.6 us (3%)
  between operations  14.5 us (2%)
    reduce_scatter x1, waiting for transfers between devices, local(): lax.psum_scatter(grad_wgu, 'row', scatter_dimension=0, tiled=True)  96.2 us
    reduce_scatter x4, waiting for transfers between devices, column_sum(): lax.psum_scatter(product(left).astype(jnp.bfloat16), 'col', scatter_dimen...  88.2 us
    unnamed x16, waiting for transfers between devices  85.8 us
    reduce_scatter x1, waiting for transfers between devices, local(): lax.psum_scatter(grad_values_all, 'row', scatter_dimension=0, tiled=True)  76.9 us
    reduce_scatter x1, waiting for transfers between devices, local(): lax.psum_scatter(grad_down, 'row', scatter_dimension=1, tiled=True)  69.8 us
    reduce_scatter x1, waiting for transfers between devices, local(): lax.psum_scatter(grad_keys_all, 'row', scatter_dimension=0, tiled=True)  68 us
    all_gather x1, waiting for transfers between devices, local(): lax.all_gather(w_gate_up, 'row', axis=0, tiled=True)  43.2 us
    psum x1, blocking collectives, local(): lax.psum((grad_gain1, grad_bias1, grad_gain2, grad_bias2), ('row', 'col'))  40.1 us
  transfers between devices with their start and end apart: 14, of which 14 were waited for; matrix products, arithmetic and copies ran while one was open for 6% of the time, Pallas kernels for 0%

commit v1 on v0

--- a/solution.py
+++ b/solution.py
@@ -156,8 +156,11 @@
     )
     value_bf = mixed[:, 2].astype(jnp.bfloat16)
     run_max = jnp.full((local_heads, group), MASKED, jnp.float32)
-    key_piece = lax.all_gather(key_bf, "row", axis=0, tiled=True)
-    value_piece = lax.all_gather(value_bf, "row", axis=0, tiled=True)
+    key_piece, value_piece = jnp.split(
+        lax.all_gather(jnp.concatenate([key_bf, value_bf], axis=1), "row", axis=0, tiled=True),
+        [key_bf.shape[1]],
+        axis=1,
+    )
     count = key_piece.shape[0]
     seg_keys = seq_all
     scores, same = score_block(query_bf, seg_rows, key_piece, seg_keys, scale)

time: 919 us -> 996 us (1.084)
  waiting for transfers between devices: 598 us -> 670 us
    all_gather x2 -> x3, waiting for transfers between devices: 33 us -> 110 us  [the longest x1 46.3 us: local(): lax.all_gather(value_bf, 'row', axis=0, tiled=True)]
    unnamed x16 -> x17, waiting for transfers between devices: 85.8 us -> 86.3 us
  transfers between devices with their start and end apart: 14 -> 15, of which waited for: 14 -> 15; matrix products, arithmetic and copies ran while one was open for 6% -> 4% of each run, Pallas kernels for 0% -> 0%
where the time goes in v1:
time: 996 us; the launch traced here: 995 us
  waiting for transfers between devices  670 us (67%)
  blocking collectives  146 us (15%)
  matrix products  99.7 us (10%)
  other arithmetic  32.1 us (3%)
  local copies, waits for them, and re-layouts  30.9 us (3%)
  between operations  14.6 us (1%)
    reduce_scatter x1, waiting for transfers between devices, local(): lax.psum_scatter(grad_wgu, 'row', scatter_dimension=0, tiled=True)  96.1 us
    unnamed x17, waiting for transfers between devices  86.3 us
    reduce_scatter x4, waiting for transfers between devices, column_sum(): lax.psum_scatter(product(left).astype(jnp.bfloat16), 'col', scatter_dimen...  85.9 us
    reduce_scatter x1, waiting for transfers between devices, local(): lax.psum_scatter(grad_values_all, 'row', scatter_dimension=0, tiled=True)  76.6 us
    reduce_scatter x1, waiting for transfers between devices, local(): lax.psum_scatter(grad_down, 'row', scatter_dimension=1, tiled=True)  69.9 us
    reduce_scatter x1, waiting for transfers between devices, local(): lax.psum_scatter(grad_keys_all, 'row', scatter_dimension=0, tiled=True)  65.5 us
    all_gather x1, waiting for transfers between devices, local(): lax.all_gather(value_bf, 'row', axis=0, tiled=True)  46.3 us
    all_gather x1, waiting for transfers between devices, local(): lax.all_gather(w_gate_up, 'row', axis=0, tiled=True)  43.3 us
  transfers between devices with their start and end apart: 15, of which 15 were waited for; matrix products, arithmetic and copies ran while one was open for 4% of the time, Pallas kernels for 0%

profile of v1, /device:TPU:0, one launch (start us, length us, event | category | flops | bytes accessed | tf_op | source)
XLA Modules:
  0.0 994.7 jit_solution(7244871201534527878)
XLA Ops:
  8.3 38.8 %all_gather.34 = bf16[768,3,192]{2,1,0:T(4,128)(2,1)S(1)} all-gather(bf16[96,3,192]{2,1,0:T(4,128)(2,1)S(1)} %copy.45), channel_id=1, replica_groups=mesh['row'=8,'col'=4] {'row'}, dimensions={0}, use_global_device_ids=true | all-gather | bytes 995328 | tf_op jit(solution)/shard_map/all_gather | solution.py:134
  49.2 8.7 all_gather.33
  62.9 34.1 %all_gather.36 = bf16[192,768]{0,1:T(8,128)(2,1)} all-gather(bf16[192,96]{0,1:T(8,128)(2,1)S(1)} %copy.47), channel_id=1, replica_groups=mesh['row'=8,'col'=4] {'row'}, dimensions={1}, use_global_device_ids=true | all-gather | bytes 331776 | tf_op jit(solution)/shard_map/all_gather | solution.py:135
  98.3 27.8 %all-gather.7.cloned.1.call-done = bf16[4096,384]{0,1:T(8,128)(2,1)} async-done(((bf16[512,384]{0,1:T(8,128)(2,1)}), bf16[4096,384]{0,1:T(8,128)(2,1)}) %all-gather.7.cloned.1.call-update) | async-done | bytes 3145744 | tf_op jit(solution)/shard_map/all_gather | solution.py:160
  128.4 11.1 %select_reduce_fusion = (f32[3,512]{1,0:T(4,128)S(1)}, f32[3,512,4096]{2,1,0:T(8,128)}) fusion(pred[512,4096]{1,0:T(8,128)(4,1)S(1)} %broadcast_compare_fusion.1, bf16[4096,3,64]{0,2,1:T(8,128)(2,1)S(1)} %bitcast.174, bf16[512,3,32]{0,2,1:T(8,128)(2,1)S(1)} %copy-done.32, bf16[512,3,32]{0,2,1:T(8,128)(2,1)S(1)} %copy-done.30), kind=kOutput, calls=%fused_computation.16 | convolution fusion | flops 824572416 | bytes 29038592 | tf_op jit(solution)/shard_map/qhd,khd->hqk/dot_general | solution.py:87
  139.6 11.9 %fusion.8 = f32[3,512]{1,0:T(4,128)S(1)} fusion(f32[3,512,4096]{2,1,0:T(8,128)} %get-tuple-element.349, f32[3,512]{1,0:T(4,128)S(1)} %broadcast_maximum_fusion, pred[512,4096]{1,0:T(8,128)(4,1)S(1)} %broadcast_compare_fusion.1), kind=kLoop, calls=%fused_computation.17 | loop fusion | flops 25164288 | bytes 27275264 | tf_op jit(solution)/shard_map/reduce_sum | solution.py:169
  151.5 11.8 %fusion.29 = (bf16[512,3,64]{0,2,1:T(8,128)(2,1)S(1)}, f32[3,512,64]{1,2,0:T(8,128)}) fusion(f32[512,3]{0,1:T(4,128)S(1)} %bitcast.187, bf16[4096,3,64]{0,2,1:T(8,128)(2,1)S(1)} %bitcast.173, f32[3,512,4096]{2,1,0:T(8,128)} %get-tuple-element.349, f32[3,512]{1,0:T(4,128)S(1)} %broadcast_maximum_fusion, pred[512,4096]{1,0:T(8,128)(4,1)S(1)} %broadcast_compare_fusion.1), kind=kOutput, calls=%fused_computation.59 | convolution fusion | flops 830668800 | bytes 29437952 | tf_op jit(solution)/shard_map/hqk,khd->hqd/dot_general | solution.py:170
  167.8 19.2 %reduce-scatter.15.cloned.1.call-done = bf16[128,768]{1,0:T(8,128)(2,1)} async-done(((bf16[512,768]{1,0:T(8,128)(2,1)}), bf16[128,768]{1,0:T(8,128)(2,1)}) %reduce-scatter.15.cloned.1.call-update) | async-done | bytes 196624 | tf_op jit(solution)/shard_map/reduce_scatter | solution.py:77
  190.2 8.4 all_gather.37
  198.6 43.3 %all-gather.9.cloned.1.call-done = bf16[768,2,768]{2,0,1:T(8,128)(2,1)} async-done(((bf16[96,2,768]{2,0,1:T(8,128)(2,1)}), bf16[768,2,768]{2,0,1:T(8,128)(2,1)}) %all-gather.9.cloned.1.call-update) | async-done | bytes 2359312 | tf_op jit(solution)/shard_map/all_gather | solution.py:136
  247.1 36.7 %all-gather.11.cloned.1.call-done = bf16[768,768]{0,1:T(8,128)(2,1)} async-done(((bf16[768,96]{0,1:T(8,128)(2,1)}), bf16[768,768]{0,1:T(8,128)(2,1)}) %all-gather.11.cloned.1.call-update) | async-done | bytes 1179664 | tf_op jit(solution)/shard_map/all_gather | solution.py:137
  286.9 22.1 %reduce-scatter.17.cloned.1.call-done = bf16[128,768]{1,0:T(8,128)(2,1)} async-done(((bf16[512,768]{1,0:T(8,128)(2,1)}), bf16[128,768]{1,0:T(8,128)(2,1)}) %reduce-scatter.17.cloned.1.call-update) | async-done | bytes 196624 | tf_op jit(solution)/shard_map/reduce_scatter | solution.py:77
  327.7 21.3 %reduce-scatter.19.cloned.1.call-done = bf16[128,768]{1,0:T(8,128)(2,1)} async-done(((bf16[512,768]{1,0:T(8,128)(2,1)}), bf16[128,768]{1,0:T(8,128)(2,1)}) %reduce-scatter.19.cloned.1.call-update) | async-done | bytes 196624 | tf_op jit(solution)/shard_map/reduce_scatter | solution.py:77
  361.6 35.5 %all-gather.13.cloned.1.call-done = bf16[4096,192]{0,1:T(8,128)(2,1)} async-done(((bf16[512,192]{0,1:T(8,128)(2,1)}), bf16[4096,192]{0,1:T(8,128)(2,1)}) %all-gather.13.cloned.1.call-update) | async-done | bytes 1572880 | tf_op jit(solution)/shard_map/all_gather | solution.py:233
  397.1 46.3 %all-gather.15.cloned.1.call-done = bf16[4096,1,192]{0,2,1:T(8,128)(2,1)} async-done(((bf16[512,1,192]{0,2,1:T(8,128)(2,1)}), bf16[4096,1,192]{0,2,1:T(8,128)(2,1)}) %all-gather.15.cloned.1.call-update) | async-done | bytes 1572880 | tf_op jit(solution)/shard_map/all_gather | solution.py:234
  447.5 58.7 %while.18 = (s32[]{:T(128)}, f32[512,3,64]{0,2,1:T(8,128)S(1)}, f32[4096,192]{0,1:T(8,128)}, f32[4096,192]{0,1:T(8,128)}, bf16[4096,192]{0,1:T(8,128)(2,1)S(1)},...) while((s32[]{:T(128)}, f32[512,3,64]{0,2,1:T(8,128)S(1)}, ...), condition=%wide.region_18.19_spmd.clone, body=%wide.region_17.18_spmd.clone.sunk | while | flops 2045968384 | bytes 107786520 | solution.py:277
  513.6 65.5 %reduce-scatter.21.cloned.1.call-done = f32[512,192]{0,1:T(8,128)} async-done(((f32[4096,192]{0,1:T(8,128)}), f32[512,192]{0,1:T(8,128)}) %reduce-scatter.21.cloned.1.call-update) | async-done | bytes 393232 | tf_op jit(solution)/shard_map/reduce_scatter | solution.py:281
  580.4 76.6 %reduce-scatter.23.cloned.1.call-done = f32[512,192]{0,1:T(8,128)} async-done(((f32[4096,192]{0,1:T(8,128)}), f32[512,192]{0,1:T(8,128)}) %reduce-scatter.23.cloned.1.call-update) | async-done | bytes 393232 | tf_op jit(solution)/shard_map/reduce_scatter | solution.py:282
  666.9 40.0 %all-reduce = (f32[768]{0:T(1024)}, f32[768]{0:T(1024)}, f32[768]{0:T(1024)}, f32[768]{0:T(1024)}) all-reduce(f32[768]{0:T(1024)S(1)} %get-tuple-element.283, f32[768]{0:T(1024)S(1)} %get-tuple-element.288, f32[768]{0:T(1024)S(1)} %copy-done.41, f32[768]{0:T(1024)S(1)} %copy-done.42), channel_id=1, replica_groups=mesh['row'=8,'col'=4] {'row','col'}, use_global_device_ids=true, to_apply=%region_27.28 | all-reduce | flops 3072 | bytes 24576 | tf_op jit(solution)/shard_map/psum | solution.py:305
  706.9 15.6 %reduce-scatter.33.cloned.1.call-done = f32[96,192]{1,0:T(8,128)} async-done(((f32[768,192]{1,0:T(8,128)}), f32[96,192]{1,0:T(8,128)}) %reduce-scatter.33.cloned.1.call-update) | async-done | bytes 73744
  724.1 96.1 %reduce-scatter.27.cloned.1.call-done = f32[96,2,768]{2,0,1:T(8,128)} async-done(((f32[768,2,768]{2,0,1:T(8,128)}), f32[96,2,768]{2,0,1:T(8,128)}) %reduce-scatter.27.cloned.1.call-update) | async-done | bytes 589840 | tf_op jit(solution)/shard_map/reduce_scatter | solution.py:302
  822.5 23.3 %reduce-scatter.25.cloned.1.call-done = bf16[128,768]{1,0:T(8,128)(2,1)} async-done(((bf16[512,768]{1,0:T(8,128)(2,1)}), bf16[128,768]{1,0:T(8,128)(2,1)}) %reduce-scatter.25.cloned.1.call-update) | async-done | bytes 196624 | tf_op jit(solution)/shard_map/reduce_scatter | solution.py:77
  847.5 68.8 %reduce-scatter.31.cloned.1.call-done = f32[96,576]{1,0:T(8,128)} async-done(((f32[768,576]{1,0:T(8,128)}), f32[96,576]{1,0:T(8,128)}) %reduce-scatter.31.cloned.1.call-update) | async-done | bytes 221200
  918.3 69.9 %reduce-scatter.29.cloned.1.call-done = f32[768,96]{0,1:T(8,128)} async-done(((f32[768,768]{0,1:T(8,128)}), f32[768,96]{0,1:T(8,128)}) %reduce-scatter.29.cloned.1.call-update) | async-done | bytes 294928 | tf_op jit(solution)/shard_map/reduce_scatter | solution.py:303
  (224 shorter events, 147.0 us)
Async XLA Ops:
  7.2 119.0 %all-gather.7.cloned.1.call-start = ((), (), s32[]{:S(2)}) async-start(), calls=%async_computation.10 | async-start | bytes 3538944 | tf_op jit(solution)/shard_map/all_gather | solution.py:160
  62.6 124.3 %reduce-scatter.15.cloned.1.call-start = ((), (), s32[]{:S(2)}) async-start(), calls=%async_computation.11 | async-start | bytes 983040 | tf_op jit(solution)/shard_map/reduce_scatter | solution.py:77
  165.4 76.6 %all-gather.9.cloned.1.call-start = ((), (), s32[]{:S(2)}) async-start(), calls=%async_computation.12 | async-start | bytes 2654208 | tf_op jit(solution)/shard_map/all_gather | solution.py:136
  167.2 116.7 %all-gather.11.cloned.1.call-start = ((), (), s32[]{:S(2)}) async-start(), calls=%async_computation.13 | async-start | bytes 1327104 | tf_op jit(solution)/shard_map/all_gather | solution.py:137
  167.7 141.3 %reduce-scatter.17.cloned.1.call-start = ((), (), s32[]{:S(2)}) async-start(), calls=%async_computation.14 | async-start | bytes 983040 | tf_op jit(solution)/shard_map/reduce_scatter | solution.py:77
  247.1 64.3 %copy-start.7 = (bf16[512,768]{1,0:T(8,128)(2,1)}, bf16[512,768]{1,0:T(8,128)(2,1)S(1)}, u32[]{:S(2)}) copy-start(bf16[512,768]{1,0:T(8,128)(2,1)S(1)} %multiply_convert_fusion.2) | copy-start | bytes 2359300
  247.1 64.2 %copy-start.43 = (f32[768]{0:T(1024)S(1)}, f32[768]{0:T(1024)}, u32[]{:S(2)}) copy-start(f32[768]{0:T(1024)} %param.22) | copy-start | bytes 9220
  286.8 62.1 %reduce-scatter.19.cloned.1.call-start = ((), (), s32[]{:S(2)}) async-start(), calls=%async_computation.15 | async-start | bytes 983040 | tf_op jit(solution)/shard_map/reduce_scatter | solution.py:77
  325.1 72.0 %all-gather.13.cloned.1.call-start = ((), (), s32[]{:S(2)}) async-start(), calls=%async_computation.16 | async-start | bytes 1769472 | tf_op jit(solution)/shard_map/all_gather | solution.py:233
  325.9 117.5 %all-gather.15.cloned.1.call-start = ((), (), s32[]{:S(2)}) async-start(), calls=%async_computation.22 | async-start | bytes 1769472 | tf_op jit(solution)/shard_map/all_gather | solution.py:234
  326.7 252.5 %reduce-scatter.21.cloned.1.call-start = ((), (), s32[]{:S(2)}) async-start(), calls=%async_computation.17 | async-start | bytes 3538944 | tf_op jit(solution)/shard_map/reduce_scatter | solution.py:281
  506.3 150.8 %reduce-scatter.23.cloned.1.call-start = ((), (), s32[]{:S(2)}) async-start(), calls=%async_computation.18 | async-start | bytes 3538944 | tf_op jit(solution)/shard_map/reduce_scatter | solution.py:282
  506.8 215.6 %reduce-scatter.33.cloned.1.call-start = ((), (), s32[]{:S(2)}) async-start(), calls=%async_computation.24 | async-start | bytes 884736
  508.8 311.4 %reduce-scatter.27.cloned.1.call-start = ((), (), s32[]{:S(2)}) async-start(), calls=%async_computation.20 | async-start | bytes 5308416 | tf_op jit(solution)/shard_map/reduce_scatter | solution.py:302
  513.5 66.7 %copy-start.26 = (f32[512,32]{0,1:T(8,128)S(1)}, f32[512,32]{0,1:T(8,128)}, u32[]{:S(2)}) copy-start(f32[512,32]{0,1:T(8,128)} %copy-done.25) | copy-start | bytes 196612
  513.5 66.7 %copy-start.28 = (f32[512,32]{0,1:T(8,128)S(1)}, f32[512,32]{0,1:T(8,128)}, u32[]{:S(2)}) copy-start(f32[512,32]{0,1:T(8,128)} %copy-done.27) | copy-start | bytes 196612
  513.5 145.2 %copy-start.9 = (bf16[768,3,192]{0,2,1:T(8,128)(2,1)S(1)}, bf16[768,3,192]{0,2,1:T(8,128)(2,1)}, u32[]{:S(2)}) copy-start(bf16[768,3,192]{0,2,1:T(8,128)(2,1)} %copy.46) | copy-start | bytes 2654212
  513.6 332.3 %reduce-scatter.25.cloned.1.call-start = ((), (), s32[]{:S(2)}) async-start(), calls=%async_computation.19 | async-start | bytes 983040 | tf_op jit(solution)/shard_map/reduce_scatter | solution.py:77
  580.4 80.2 %copy-start.33 = (bf16[512,3,64]{0,2,1:T(8,128)(2,1)}, bf16[512,3,64]{0,2,1:T(8,128)(2,1)S(1)}, u32[]{:S(2)}) copy-start(bf16[512,3,64]{0,2,1:T(8,128)(2,1)S(1)} %pad_maximum_fusion.9) | copy-start | bytes 589828
  580.4 80.4 %copy-start.15 = (bf16[512,768]{1,0:T(8,128)(2,1)S(1)}, bf16[512,768]{1,0:T(8,128)(2,1)}, u32[]{:S(2)}) copy-start(bf16[512,768]{1,0:T(8,128)(2,1)} %copy-done.14) | copy-start | bytes 2359300
  580.4 80.1 %copy-start.34 = (bf16[512,3,64]{0,2,1:T(8,128)(2,1)}, bf16[512,3,64]{0,2,1:T(8,128)(2,1)S(1)}, u32[]{:S(2)}) copy-start(bf16[512,3,64]{0,2,1:T(8,128)(2,1)S(1)} %pad_maximum_fusion.10) | copy-start | bytes 589828
  660.6 255.7 %reduce-scatter.31.cloned.1.call-start = ((), (), s32[]{:S(2)}) async-start(), calls=%async_computation.23 | async-start | bytes 2211840
  664.4 323.7 %reduce-scatter.29.cloned.1.call-start = ((), (), s32[]{:S(2)}) async-start(), calls=%async_computation.21 | async-start | bytes 2654208 | tf_op jit(solution)/shard_map/reduce_scatter | solution.py:303
  666.8 179.0 %copy-start.19 = (f32[128,768]{1,0:T(8,128)S(1)}, f32[128,768]{1,0:T(8,128)}, u32[]{:S(2)}) copy-start(f32[128,768]{1,0:T(8,128)} %get-tuple-element.320) | copy-start | bytes 1179652
  (43 other events, 524.7 us)
Sparse Core Ops, SparseCore 0:
  62.8 63.3 all-gather.6
  165.5 21.4 reduce-scatter.14
  190.0 51.9 all-gather.8
  244.2 39.5 all-gather.10
  286.9 22.0 reduce-scatter.16
  325.2 23.6 reduce-scatter.18
  351.7 45.3 all-gather.12
  399.9 43.4 all-gather.14
  506.4 72.7 reduce-scatter.20
  583.1 73.9 reduce-scatter.22
  660.7 61.6 reduce-scatter.32
  726.0 94.1 reduce-scatter.26
  822.7 23.0 reduce-scatter.24
  849.6 66.7 reduce-scatter.30
  920.2 67.9 reduce-scatter.28
